TPU v7x, 128 devices: a whole 4x4x4 slice. The times are simulated.
128 devices in a mesh: row: 8 (over x_lo, z), col: 16 (over x_hi, y, core).
Axes of the slice: x: 4 (x_hi: 2, x_lo: 2; x = x_hi * 2 + x_lo), y: 4, z: 4, core: 2. Of those that a mesh axis runs over, the one named last changes fastest.
Arguments:
- ancestor: float32 [24576, 24576], P('row', 'col'), may hold values from -6 to 6
- lhat_one: float32 [24576, 512], P('col', 'row'), may hold values from -0.15625 to 0.15625
- lhat_two: float32 [24576, 512], P('col', 'row'), may hold values from -0.15625 to 0.15625
- link_two: float32 [512, 512], replicated, may hold values from -0.25 to 0.25
- diag_one: float32 [512, 512], replicated, may hold values from -6 to 6
- diag_two: float32 [512, 512], replicated, may hold values from -6 to 6
- mask_one: int32 [192], replicated, may hold values from 0 to 1, as said below
- mask_two: int32 [192], replicated, may hold values from 0 to 1, as said below
Outputs:
- x_one: float32 [24576, 512], P('row', 'col')
- d_one: float32 [512, 512], replicated
- x_two: float32 [24576, 512], P('row', 'col')
- link_inverse: float32 [512, 512], replicated
- d_two: float32 [512, 512], replicated
Inputs may be any that keep to these rules, and one draw needn't show every extreme that they name: `mask_one`: 1 where a block of 128 factor rows is nonzero, else 0; the last block is always nonzero. `mask_two`: 1 where a block of 128 factor rows is nonzero, else 0; the last block is always nonzero.
All inputs are finite; a program needn't handle non-finite values.
Results may differ from a plain program's by a relative error of at most 0.00011.
Values sent between devices are 32-bit elements; how exact they have to be, the bound alone decides.
No kernel may reach another device: no remote copies, remote signals or barrier semaphores. Data moves between devices by JAX's collectives and lax.ppermute only.
A program may use at most 128 MiB of HBM per device.

v0:
```python
import jax
import jax.numpy as jnp
from jax import lax
from jax.sharding import Mesh, PartitionSpec as P

BLOCK = 128
ROW = ("xl", "z")
COL = ("xh", "y", "core")
ALL = ROW + COL
SIZES = (2, 4, 2, 4, 2)
SWAP = ((0, 1), (1, 0))


def product(left, right, contract=((1,), (0,))):
    return lax.dot_general(
        left,
        right,
        (contract, ((), ())),
        precision=lax.Precision.HIGH,
        preferred_element_type=jnp.float32,
    )


def linear(xl, z, xh, y, core):
    return (((xl * 4 + z) * 2 + xh) * 4 + y) * 2 + core


def factor_routes():
    routes = []
    for xl in range(2):
        for z in range(4):
            for xh in range(2):
                for y in range(4):
                    for core in range(2):
                        source = linear(y // 2, y % 2 * 2 + core, xl, z, xh)
                        routes.append((source, linear(xl, z, xh, y, core)))
    return routes


def per_device(ancestor, lhat_one, lhat_two, link_two, diag_one, diag_two, mask_one, mask_two):
    row_index = lax.axis_index(ROW)
    column_index = lax.axis_index(COL)
    core = lax.axis_index("core")
    xh = lax.axis_index("xh")
    rows, depth = ancestor.shape
    width = link_two.shape[0]
    blocks = depth // BLOCK
    part = rows // 16

    def masked(shard, mask):
        own = lax.dynamic_slice_in_dim(mask, column_index * blocks, blocks).astype(jnp.float32)
        return (shard.reshape(blocks, BLOCK, -1) * own[:, None, None]).reshape(shard.shape)

    def row_sum(factor):
        partial = product(ancestor, factor).reshape(2, 4, 2, part, width)
        keep = lax.dynamic_index_in_dim(partial, core, 2, keepdims=False)
        send = lax.dynamic_index_in_dim(partial, 1 - core, 2, keepdims=False)
        chip = keep + lax.ppermute(send, "core", SWAP)
        chip = chip.transpose(1, 0, 2, 3).reshape(8 * part, width)
        line = lax.psum_scatter(chip, "y", scatter_dimension=0, tiled=True).reshape(2, part, width)
        own = lax.dynamic_index_in_dim(line, xh, 0, keepdims=False)
        other = lax.dynamic_index_in_dim(line, 1 - xh, 0, keepdims=False)
        return own + lax.ppermute(other, "xh", SWAP)

    factor_one = lax.all_gather(masked(lhat_one, mask_one), ROW, axis=1, tiled=True)
    factor_two = lax.all_gather(masked(lhat_two, mask_two), ROW, axis=1, tiled=True)
    local = jnp.concatenate(
        [lax.dynamic_slice_in_dim(f, row_index * part, part, 0) for f in (factor_one, factor_two)],
        axis=1,
    )
    local = lax.ppermute(local, ALL, factor_routes())
    sum_one = row_sum(factor_one)
    sum_two = row_sum(factor_two)
    gram_one = product(local, sum_one, ((0,), (0,)))
    gram_two = product(local[:, width:], sum_two, ((0,), (0,)))
    grams = jnp.concatenate([gram_one, gram_two], axis=0)
    half = grams.shape[0] // 2
    keep = lax.dynamic_slice_in_dim(grams, core * half, half, 0)
    send = lax.dynamic_slice_in_dim(grams, (1 - core) * half, half, 0)
    piece = keep + lax.ppermute(send, "core", SWAP)
    piece = lax.psum_scatter(piece, "y", scatter_dimension=0, tiled=True)
    piece = lax.psum_scatter(piece, "z", scatter_dimension=0, tiled=True)
    piece = lax.psum(piece, ("xl", "xh"))
    piece = lax.all_gather(piece, "z", axis=0, tiled=True)
    piece = lax.all_gather(piece, "y", axis=0, tiled=True)
    other = lax.ppermute(piece, "core", SWAP)
    grams = jnp.where(
        core == 0, jnp.concatenate([piece, other], 0), jnp.concatenate([other, piece], 0)
    )
    cross = grams[width : 2 * width]
    d_one = diag_one + grams[:width]
    link_inverse = cross.T - product(d_one, link_two)
    d_two = (
        diag_two
        + grams[2 * width :]
        - product(cross, link_two)
        - product(link_two, link_inverse, ((0,), (0,)))
    )
    own_two = product(sum_one, link_two) - sum_two
    out = jnp.stack([-sum_one, own_two], axis=0)
    out = lax.all_to_all(out, COL, split_axis=2, concat_axis=1, tiled=True)
    return (out[0], d_one, out[1], link_inverse, d_two)


def solution(mesh):
    fine = Mesh(mesh.devices.reshape(SIZES), ALL)
    in_specs = (P(ROW, COL), P(COL, ROW), P(COL, ROW), P(), P(), P(), P(), P())
    out_specs = (P(ROW, COL), P(), P(ROW, COL), P(), P())
    return jax.shard_map(
        per_device, mesh=fine, in_specs=in_specs, out_specs=out_specs, check_vma=False
    )
```

profile of v0, /device:TPU:1, one launch (start us, length us, event | category | flops | bytes accessed | tf_op | source)
XLA Modules:
  0.0 407.2 jit_solution(15928660699130049153)
XLA Ops:
  7.2 0.8 dynamic-slice_convert_fusion
  8.1 0.1 broadcast_bitcast_fusion.1
  8.2 1.8 broadcast_multiply_fusion.1
  10.0 0.0 all-gather.6.cloned.1.call-start
  10.0 0.1 broadcast_bitcast_fusion
  10.1 1.8 broadcast_multiply_fusion
  11.9 43.3 %all-gather.4.cloned.1.call-done = f32[1536,512]{0,1:T(8,128)} async-done(((f32[1536,64]{0,1:T(8,128)}), f32[1536,512]{0,1:T(8,128)}) %all-gather.4.cloned.1.call-update) | async-done | bytes 3145744 | tf_op jit(solution)/shard_map/all_gather | solution.py:65
  55.2 20.6 %convolution_bitcast_fusion.1 = f32[3072,512]{0,1:T(8,128)} fusion(f32[1536,512]{0,1:T(8,128)} %all-gather.4.cloned.1.call-done, f32[3072,1536]{1,0:T(8,128)} %param.8), kind=kOutput, calls=%fused_computation.1 | convolution fusion | flops 14495514624 | bytes 28311552 | tf_op jit(solution)/shard_map/dot_general | solution.py:15
  75.8 6.6 %copy.48 = f32[3072,512]{1,0:T(8,128)} copy(f32[3072,512]{0,1:T(8,128)} %convolution_bitcast_fusion.1) | data formatting | bytes 12582912 | tf_op jit(solution)/shard_map/dot_general | solution.py:15
  82.5 3.9 dynamic-slice_bitcast_fusion.1
  86.4 3.0 collective-permute-start
  89.4 5.6 %collective-permute-done = f32[2,4,192,512]{3,2,1,0:T(8,128)} collective-permute-done((f32[2,4,192,512]{3,2,1,0:T(8,128)}, f32[2,4,192,512]{3,2,1,0:T(8,128)}, u32[]{:S(2)}, u32[]{:S(2)}) %collective-permute-start) | collective-permute-done | bytes 3145760 | tf_op jit(solution)/shard_map/ppermute | solution.py:58
  95.1 3.6 fusion.1
  98.7 2.0 copy.49
  100.8 0.0 reduce-scatter.7.cloned.1.call-start
  100.8 0.5 all-gather.6.cloned.1.call-done
  101.3 20.6 %convolution_bitcast_fusion = f32[3072,512]{0,1:T(8,128)} fusion(f32[1536,512]{0,1:T(8,128)} %all-gather.6.cloned.1.call-done, f32[3072,1536]{1,0:T(8,128)} %param.8), kind=kOutput, calls=%fused_computation | convolution fusion | flops 14495514624 | bytes 28311552 | tf_op jit(solution)/shard_map/dot_general | solution.py:15
  121.9 6.6 %copy.50 = f32[3072,512]{1,0:T(8,128)} copy(f32[3072,512]{0,1:T(8,128)} %convolution_bitcast_fusion) | data formatting | bytes 12582912 | tf_op jit(solution)/shard_map/dot_general | solution.py:15
  128.5 2.4 dynamic-slice_bitcast_fusion
  130.9 3.3 collective-permute-start.2
  134.2 5.3 %collective-permute-done.2 = f32[2,4,192,512]{3,2,1,0:T(8,128)S(1)} collective-permute-done((f32[2,4,192,512]{3,2,1,0:T(8,128)S(1)}, f32[2,4,192,512]{3,2,1,0:T(8,128)S(1)}, u32[]{:S(2)}, u32[]{:S(2)}) %collective-permute-start.2) | collective-permute-done | bytes 3145760 | tf_op jit(solution)/shard_map/ppermute | solution.py:58
  139.5 0.7 fusion
  140.3 1.9 copy.51
  142.3 1.3 constant_dynamic-slice_fusion
  143.6 1.4 constant_dynamic-slice_fusion.1
  145.0 0.1 pad_maximum_fusion
  145.1 0.3 copy.55
  145.4 4.6 %collective-permute-start.4 = (f32[192,1024]{1,0:T(8,128)S(1)}, f32[192,1024]{1,0:T(8,128)S(1)}, u32[]{:S(2)}, u32[]{:S(2)}) collective-permute-start(f32[192,1024]{1,0:T(8,128)S(1)} %copy.55), channel_id=1, source_target_pairs={{0,0},{16,1},{32,2},{48,3},{64,4},{80,5},{96,6},{112,7},{1,8},{17,... | collective-permute-start | bytes 2359304 | tf_op jit(solution)/shard_map/ppermute | solution.py:71
  150.1 1.0 dynamic-slice_bitcast_fusion.3
  151.1 0.6 collective-permute-start.1
  151.7 44.6 %reduce-scatter.7.cloned.1.call-done = f32[384,512]{1,0:T(8,128)} async-done(((f32[1536,512]{1,0:T(8,128)}), f32[384,512]{1,0:T(8,128)}) %reduce-scatter.7.cloned.1.call-update) | async-done | bytes 786448 | tf_op jit(solution)/shard_map/reduce_scatter | solution.py:60
  196.3 1.8 dynamic-slice_bitcast_fusion.2
  198.1 4.6 %collective-permute-start.3 = (f32[192,512]{1,0:T(8,128)}, f32[192,512]{1,0:T(8,128)S(1)}, u32[]{:S(2)}, u32[]{:S(2)}) collective-permute-start(f32[192,512]{1,0:T(8,128)} %dynamic-slice_bitcast_fusion.2), channel_id=1, source_target_pairs={{0,8},{8,0},{1,9},{9,1},{2,10},{10,2},{3,11},{11,3},{4,12},{12,4},... | collective-permute-start | bytes 1179656 | tf_op jit(solution)/shard_map/ppermute | solution.py:63
  202.7 1.9 negate_bitcast_fusion
  204.6 7.3 %collective-permute-done.3 = f32[192,512]{1,0:T(8,128)S(1)} collective-permute-done((f32[192,512]{1,0:T(8,128)}, f32[192,512]{1,0:T(8,128)S(1)}, u32[]{:S(2)}, u32[]{:S(2)}) %collective-permute-start.3) | collective-permute-done | bytes 393248 | tf_op jit(solution)/shard_map/ppermute | solution.py:63
  212.0 1.8 fusion.10
  213.8 2.6 fusion.14
  216.4 1.7 fusion.2
  218.1 1.0 collective-permute-start.5
  219.1 3.4 collective-permute-done.5
  222.5 3.4 fusion.4
  226.0 25.9 %reduce-scatter.9.cloned.1.call-done = f32[192,512]{1,0:T(8,128)} async-done(((f32[768,512]{1,0:T(8,128)}), f32[192,512]{1,0:T(8,128)}) %reduce-scatter.9.cloned.1.call-update) | async-done | bytes 393232 | tf_op jit(solution)/shard_map/reduce_scatter | solution.py:81
  252.0 21.9 %reduce-scatter.11.cloned.1.call-done = f32[48,512]{1,0:T(8,128)} async-done(((f32[192,512]{1,0:T(8,128)}), f32[48,512]{1,0:T(8,128)}) %reduce-scatter.11.cloned.1.call-update) | async-done | bytes 98320 | tf_op jit(solution)/shard_map/reduce_scatter | solution.py:82
  273.9 43.5 %all-reduce.2.cloned.1.call-done = f32[48,512]{1,0:T(8,128)} async-done(((f32[48,512]{1,0:T(8,128)}), f32[48,512]{1,0:T(8,128)}) %all-reduce.2.cloned.1.call-update) | async-done | bytes 98320 | tf_op jit(solution)/shard_map/psum | solution.py:83
  317.4 12.7 %all_gather.14 = f32[192,512]{1,0:T(8,128)} all-gather(f32[48,512]{1,0:T(8,128)} %all-reduce.2.cloned.1.call-done), channel_id=1, replica_groups=mesh['xl'=2,'z'=4,'xh'=2,'y'=4,'core'=2] {'z'}, dimensions={0}, use_global_device_ids=true | all-gather | bytes 491520 | tf_op jit(solution)/shard_map/all_gather | solution.py:84
  330.1 30.0 %all-gather.8.cloned.1.call-done = f32[768,512]{1,0:T(8,128)} async-done(((f32[192,512]{1,0:T(8,128)}), f32[768,512]{1,0:T(8,128)}) %all-gather.8.cloned.1.call-update) | async-done | bytes 1572880 | tf_op jit(solution)/shard_map/all_gather | solution.py:85
  360.1 0.8 collective-permute-start.6
  360.9 0.5 fusion.5
  361.4 0.1 pad_maximum_fusion.1
  361.5 1.3 copy.52
  362.8 5.5 %all-to-all-start = ((f32[2,192,512]{1,0,2:T(2,128)}), f32[2,192,512]{1,0,2:T(2,128)S(1)}, u32[]{:S(2)}, u32[]{:S(2)}) async-start(f32[2,192,512]{1,0,2:T(2,128)} %copy.52), calls=%async_computation.2 | async-start | bytes 2097152 | tf_op jit(solution)/shard_map/all_to_all | solution.py:101
  368.3 17.1 %all-to-all-done = f32[2,192,512]{1,0,2:T(2,128)S(1)} async-done(((f32[2,192,512]{1,0,2:T(2,128)}), f32[2,192,512]{1,0,2:T(2,128)S(1)}, u32[]{:S(2)}, u32[]{:S(2)}) %all-to-all-start) | async-done | bytes 786464 | tf_op jit(solution)/shard_map/all_to_all | solution.py:101
  385.4 0.1 copy.53
  385.5 0.1 fusion.13
  385.6 0.3 copy.54
  385.9 1.0 squeeze.40
  386.9 0.3 copy.56
  387.2 1.0 squeeze.41
  388.1 3.7 maximum_select_fusion
  391.8 2.0 fusion.8
  393.8 0.2 slice_add_fusion.1
  394.0 1.1 bitcast_subtract_fusion
  395.1 1.3 copy.59
  396.4 3.9 fusion.7
  (40 shorter events, 0.5 us)
Async XLA Ops:
  7.2 353.7 %copy-start = (f32[512,512]{1,0:T(8,128)S(1)}, f32[512,512]{1,0:T(8,128)}, u32[]{:S(2)}) copy-start(f32[512,512]{1,0:T(8,128)} %param.11) | copy-start | bytes 3145732
  7.2 48.0 %all-gather.4.cloned.1.call-start = ((), (), s32[]{:S(2)}) async-start(), calls=%async_computation.5 | async-start | bytes 3538944 | tf_op jit(solution)/shard_map/all_gather | solution.py:65
  10.0 91.3 %all-gather.6.cloned.1.call-start = ((), (), s32[]{:S(2)}) async-start(), calls=%async_computation.7 | async-start | bytes 3538944 | tf_op jit(solution)/shard_map/all_gather | solution.py:66
  11.9 138.2 %reduce-scatter.5.cloned.1.call-start = ((), (), s32[]{:S(2)}) async-start(), calls=%async_computation.6 | async-start | bytes 3932160 | tf_op jit(solution)/shard_map/reduce_scatter | solution.py:60
  86.4 8.7 %collective-permute-start = (f32[2,4,192,512]{3,2,1,0:T(8,128)}, f32[2,4,192,512]{3,2,1,0:T(8,128)}, u32[]{:S(2)}, u32[]{:S(2)}) collective-permute-start(f32[2,4,192,512]{3,2,1,0:T(8,128)} %dynamic-slice_bitcast_fusion.1), channel_id=1, source_target_pairs={{0,1},{1,0},{2,3},{3,2},{4,5},{5,4},{6,7},{7,6},{8,9},{9,8},{10,11... | collective-permute-start | bytes 9437192 | tf_op jit(solution)/shard_map/ppermute | solution.py:58
  100.8 95.5 %reduce-scatter.7.cloned.1.call-start = ((), (), s32[]{:S(2)}) async-start(), calls=%async_computation.8 | async-start | bytes 3932160 | tf_op jit(solution)/shard_map/reduce_scatter | solution.py:60
  128.5 11.0 %copy-start.1 = (f32[3072,512]{1,0:T(8,128)S(1)}, f32[3072,512]{1,0:T(8,128)}, u32[]{:S(2)}) copy-start(f32[3072,512]{1,0:T(8,128)} %copy.50) | copy-start | bytes 18874372
  130.9 8.6 %collective-permute-start.2 = (f32[2,4,192,512]{3,2,1,0:T(8,128)S(1)}, f32[2,4,192,512]{3,2,1,0:T(8,128)S(1)}, u32[]{:S(2)}, u32[]{:S(2)}) collective-permute-start(f32[2,4,192,512]{3,2,1,0:T(8,128)S(1)} %dynamic-slice_bitcast_fusion), channel_id=1, source_target_pairs={{0,1},{1,0},{2,3},{3,2},{4,5},{5,4},{6,7},{7,6},{8,9},{9,8},{10,11... | collective-permute-start | bytes 9437192 | tf_op jit(solution)/shard_map/ppermute | solution.py:58
  142.2 109.7 %reduce-scatter.9.cloned.1.call-start = ((), (), s32[]{:S(2)}) async-start(), calls=%async_computation.9 | async-start | bytes 1966080 | tf_op jit(solution)/shard_map/reduce_scatter | solution.py:81
  145.4 59.2 %collective-permute-start.4 = (f32[192,1024]{1,0:T(8,128)S(1)}, f32[192,1024]{1,0:T(8,128)S(1)}, u32[]{:S(2)}, u32[]{:S(2)}) collective-permute-start(f32[192,1024]{1,0:T(8,128)S(1)} %copy.55), channel_id=1, source_target_pairs={{0,0},{16,1},{32,2},{48,3},{64,4},{80,5},{96,6},{112,7},{1,8},{17,... | collective-permute-start | bytes 2359304 | tf_op jit(solution)/shard_map/ppermute | solution.py:71
  151.1 51.6 %collective-permute-start.1 = (f32[192,512]{1,0:T(8,128)S(1)}, f32[192,512]{1,0:T(8,128)}, u32[]{:S(2)}, u32[]{:S(2)}) collective-permute-start(f32[192,512]{1,0:T(8,128)S(1)} %dynamic-slice_bitcast_fusion.3), channel_id=1, source_target_pairs={{0,8},{8,0},{1,9},{9,1},{2,10},{10,2},{3,11},{11,3},{4,12},{12,4},... | collective-permute-start | bytes 1179656 | tf_op jit(solution)/shard_map/ppermute | solution.py:63
  198.1 13.9 %collective-permute-start.3 = (f32[192,512]{1,0:T(8,128)}, f32[192,512]{1,0:T(8,128)S(1)}, u32[]{:S(2)}, u32[]{:S(2)}) collective-permute-start(f32[192,512]{1,0:T(8,128)} %dynamic-slice_bitcast_fusion.2), channel_id=1, source_target_pairs={{0,8},{8,0},{1,9},{9,1},{2,10},{10,2},{3,11},{11,3},{4,12},{12,4},... | collective-permute-start | bytes 1179656 | tf_op jit(solution)/shard_map/ppermute | solution.py:63
  204.6 9.2 %copy-start.5 = (f32[192,1024]{1,0:T(8,128)}, f32[192,1024]{1,0:T(8,128)S(1)}, u32[]{:S(2)}) copy-start(f32[192,1024]{1,0:T(8,128)S(1)} %collective-permute-done.4) | copy-start | bytes 2359300
  212.0 1.8 copy-start.7
  213.8 4.3 %copy-start.3 = (f32[512,512]{1,0:T(8,128)}, f32[512,512]{1,0:T(8,128)S(1)}, u32[]{:S(2)}) copy-start(f32[512,512]{1,0:T(8,128)S(1)} %fusion.10) | copy-start | bytes 3145732
  218.1 4.4 %collective-permute-start.5 = (f32[768,512]{1,0:T(8,128)}, f32[768,512]{1,0:T(8,128)}, u32[]{:S(2)}, u32[]{:S(2)}) collective-permute-start(f32[768,512]{1,0:T(8,128)} %fusion.2), channel_id=1, source_target_pairs={{0,1},{1,0},{2,3},{3,2},{4,5},{5,4},{6,7},{7,6},{8,9},{9,8},{10,11... | collective-permute-start | bytes 4718600 | tf_op jit(solution)/shard_map/ppermute | solution.py:80
  226.0 135.0 %copy-start.6 = (f32[384,512]{1,0:T(8,128)S(1)}, f32[384,512]{1,0:T(8,128)}, u32[]{:S(2)}) copy-start(f32[384,512]{1,0:T(8,128)} %reduce-scatter.7.cloned.1.call-done) | copy-start | bytes 2359300
  226.0 135.0 %copy-start.8 = (f32[192,512]{1,0:T(8,128)S(1)}, f32[192,512]{1,0:T(8,128)}, u32[]{:S(2)}) copy-start(f32[192,512]{1,0:T(8,128)} %copy-done.7) | copy-start | bytes 1179652
  226.0 135.5 %copy-start.9 = (f32[1,192,512]{2,1,0:T(8,128)S(1)}, f32[1,192,512]{2,1,0:T(8,128)}, u32[]{:S(2)}) copy-start(f32[1,192,512]{2,1,0:T(8,128)} %get-tuple-element.30) | copy-start | bytes 1179652
  226.0 47.8 %reduce-scatter.11.cloned.1.call-start = ((), (), s32[]{:S(2)}) async-start(), calls=%async_computation.10 | async-start | bytes 491520 | tf_op jit(solution)/shard_map/reduce_scatter | solution.py:82
  251.9 65.4 %all-reduce.2.cloned.1.call-start = ((), (), s32[]{:S(2)}) async-start(), calls=%async_computation.11 | async-start | bytes 196608 | tf_op jit(solution)/shard_map/psum | solution.py:83
  273.9 86.2 %all-gather.8.cloned.1.call-start = ((), (), s32[]{:S(2)}) async-start(), calls=%async_computation.12 | async-start | bytes 1966080 | tf_op jit(solution)/shard_map/all_gather | solution.py:85
  360.1 28.1 %collective-permute-start.6 = (f32[768,512]{1,0:T(8,128)}, f32[768,512]{1,0:T(8,128)}, u32[]{:S(2)}, u32[]{:S(2)}) collective-permute-start(f32[768,512]{1,0:T(8,128)} %all-gather.8.cloned.1.call-done), channel_id=1, source_target_pairs={{0,1},{1,0},{2,3},{3,2},{4,5},{5,4},{6,7},{7,6},{8,9},{9,8},{10,11... | collective-permute-start | bytes 4718600 | tf_op jit(solution)/shard_map/ppermute | solution.py:86
  362.8 22.6 %all-to-all-start = ((f32[2,192,512]{1,0,2:T(2,128)}), f32[2,192,512]{1,0,2:T(2,128)S(1)}, u32[]{:S(2)}, u32[]{:S(2)}) async-start(f32[2,192,512]{1,0,2:T(2,128)} %copy.52), calls=%async_computation.2 | async-start | bytes 2097152 | tf_op jit(solution)/shard_map/all_to_all | solution.py:101
  391.8 2.2 copy-start.2
  391.8 2.0 copy-start.10
  394.0 2.4 copy-start.4
Sparse Core Ops, SparseCore 0:
  10.2 44.9 all-gather.3
  57.4 43.7 all-gather.5
  103.7 40.2 reduce-scatter.4
  146.2 50.0 reduce-scatter.6
  226.1 25.7 reduce-scatter.8
  254.2 19.6 reduce-scatter.10
  276.1 41.1 all-reduce.1
  330.2 29.8 all-gather.7
where the time goes:
time: 408 us; the launch traced here: 407 us
  waiting for transfers between devices  248 us (61%)
  matrix products  53.1 us (13%)
  local copies, waits for them, and re-layouts  34.9 us (9%)
  starting transfers between devices  23.8 us (6%)
  other arithmetic  19.8 us (5%)
  between operations  14.4 us (4%)
  blocking collectives  12.7 us (3%)
    dot_general x8, matrix products, product(): lax.dot_general(left, right, (contract, ((), ())), precision=lax.Precisio...  53.1 us
    reduce_scatter x2, waiting for transfers between devices, row_sum(): lax.psum_scatter(chip, 'y', scatter_dimension=0, tiled=True)  44.6 us
    psum x1, waiting for transfers between devices, per_device(): piece = lax.psum(piece, ('xl', 'xh'))  43.5 us
    all_gather x1, waiting for transfers between devices, per_device(): lax.all_gather(masked(lhat_one, mask_one), ROW, axis=1, tiled=True)  43.3 us
    all_gather x1, waiting for transfers between devices, per_device(): piece = lax.all_gather(piece, 'y', axis=0, tiled=True)  30 us
    reduce_scatter x1, waiting for transfers between devices, per_device(): piece = lax.psum_scatter(piece, 'y', scatter_dimension=0, tiled=True)  25.9 us
    reduce_scatter x1, waiting for transfers between devices, per_device(): piece = lax.psum_scatter(piece, 'z', scatter_dimension=0, tiled=True)  21.9 us
    all_to_all x1, waiting for transfers between devices, per_device(): out = lax.all_to_all(out, COL, split_axis=2, concat_axis=1, tiled=True)  17.1 us
  transfers between devices with their start and end apart: 16, of which 12 were waited for; matrix products, arithmetic and copies ran while one was open for 20% of the time, Pallas kernels for 0%

commit v1 on v0

--- a/solution.py
+++ b/solution.py
@@ -80,7 +80,7 @@
     piece = keep + lax.ppermute(send, "core", SWAP)
     piece = lax.psum_scatter(piece, "y", scatter_dimension=0, tiled=True)
     piece = lax.psum_scatter(piece, "z", scatter_dimension=0, tiled=True)
-    piece = lax.psum(piece, ("xl", "xh"))
+    piece = jnp.sum(lax.all_gather(piece, ("xl", "xh")), axis=0)
     piece = lax.all_gather(piece, "z", axis=0, tiled=True)
     piece = lax.all_gather(piece, "y", axis=0, tiled=True)
     other = lax.ppermute(piece, "core", SWAP)

time: 408 us -> 385 us (0.944)
  waiting for transfers between devices: 248 us -> 203 us
  local copies, waits for them, and re-layouts: 34.9 us -> 47.1 us
  blocking collectives: 12.7 us -> 22.5 us
    psum x1 -> x0, waiting for transfers between devices: 43.5 us -> none  [per_device(): piece = lax.psum(piece, ('xl', 'xh'))]
    all_gather x0 -> x1, blocking collectives: none -> 11.9 us  [per_device(): piece = jnp.sum(lax.all_gather(piece, ('xl', 'xh')), axis=0)]
    unnamed x23 -> x20, local copies, waits for them, and re-layouts: 1.36 us -> 8.66 us
    all_to_all x1, waiting for transfers between devices: 17.1 us -> 12.1 us  [per_device(): out = lax.all_to_all(out, COL, split_axis=2, concat_axis=1, tiled=True)]
  transfers between devices with their start and end apart: 16 -> 15, of which waited for: 12 -> 11; matrix products, arithmetic and copies ran while one was open for 20% -> 24% of each run, Pallas kernels for 0% -> 0%
where the time goes in v1:
time: 385 us; the launch traced here: 384 us
  waiting for transfers between devices  203 us (53%)
  matrix products  53.1 us (14%)
  local copies, waits for them, and re-layouts  47.1 us (12%)
  starting transfers between devices  23.9 us (6%)
  blocking collectives  22.5 us (6%)
  other arithmetic  19.6 us (5%)
  between operations  14.4 us (4%)
    dot_general x8, matrix products, product(): lax.dot_general(left, right, (contract, ((), ())), precision=lax.Precisio...  53.1 us
    reduce_scatter x2, waiting for transfers between devices, row_sum(): lax.psum_scatter(chip, 'y', scatter_dimension=0, tiled=True)  44.6 us
    all_gather x1, waiting for transfers between devices, per_device(): lax.all_gather(masked(lhat_one, mask_one), ROW, axis=1, tiled=True)  43.3 us
    all_gather x1, waiting for transfers between devices, per_device(): piece = lax.all_gather(piece, 'y', axis=0, tiled=True)  33.3 us
    reduce_scatter x1, waiting for transfers between devices, per_device(): piece = lax.psum_scatter(piece, 'y', scatter_dimension=0, tiled=True)  25.9 us
    reduce_scatter x1, waiting for transfers between devices, per_device(): piece = lax.psum_scatter(piece, 'z', scatter_dimension=0, tiled=True)  21.8 us
    dot_general x2, local copies, waits for them, and re-layouts, product(): lax.dot_general(left, right, (contract, ((), ())), precision=lax.Precisio...  13.2 us
    all_to_all x1, waiting for transfers between devices, per_device(): out = lax.all_to_all(out, COL, split_axis=2, concat_axis=1, tiled=True)  12.1 us
  transfers between devices with their start and end apart: 15, of which 11 were waited for; matrix products, arithmetic and copies ran while one was open for 24% of the time, Pallas kernels for 0%

profile of v1, /device:TPU:1, one launch (start us, length us, event | category | flops | bytes accessed | tf_op | source)
XLA Modules:
  0.0 383.9 jit_solution(13337004832124991004)
XLA Ops:
  7.2 0.8 dynamic-slice_convert_fusion
  8.2 1.8 broadcast_multiply_fusion.1
  10.1 1.8 broadcast_multiply_fusion
  11.9 43.3 %all-gather.5.cloned.1.call-done = f32[1536,512]{0,1:T(8,128)} async-done(((f32[1536,64]{0,1:T(8,128)}), f32[1536,512]{0,1:T(8,128)}) %all-gather.5.cloned.1.call-update) | async-done | bytes 3145744 | tf_op jit(solution)/shard_map/all_gather | solution.py:65
  55.2 20.6 %convolution_bitcast_fusion.1 = f32[3072,512]{0,1:T(8,128)} fusion(f32[1536,512]{0,1:T(8,128)} %all-gather.5.cloned.1.call-done, f32[3072,1536]{1,0:T(8,128)} %param.8), kind=kOutput, calls=%fused_computation.1 | convolution fusion | flops 14495514624 | bytes 28311552 | tf_op jit(solution)/shard_map/dot_general | solution.py:15
  75.8 6.6 %copy.59 = f32[3072,512]{1,0:T(8,128)} copy(f32[3072,512]{0,1:T(8,128)} %convolution_bitcast_fusion.1) | data formatting | bytes 12582912 | tf_op jit(solution)/shard_map/dot_general | solution.py:15
  82.5 3.9 %dynamic-slice_bitcast_fusion.1 = f32[2,4,192,512]{3,2,1,0:T(8,128)} fusion(f32[2,4,2,192,512]{4,3,2,1,0:T(8,128)} %bitcast.75, s32[]{:T(128)S(6)} %select_n.42), kind=kLoop, calls=%fused_computation.12 | loop fusion | bytes 6291460 | tf_op jit(solution)/shard_map/jit(dynamic_index_in_dim)/squeeze | solution.py:57
  86.4 3.0 collective-permute-start
  89.4 5.6 %collective-permute-done = f32[2,4,192,512]{3,2,1,0:T(8,128)} collective-permute-done((f32[2,4,192,512]{3,2,1,0:T(8,128)}, f32[2,4,192,512]{3,2,1,0:T(8,128)}, u32[]{:S(2)}, u32[]{:S(2)}) %collective-permute-start) | collective-permute-done | bytes 3145760 | tf_op jit(solution)/shard_map/ppermute | solution.py:58
  95.1 3.6 fusion.1
  98.7 2.0 copy.60
  100.8 0.5 all-gather.7.cloned.1.call-done
  101.3 20.6 %convolution_bitcast_fusion = f32[3072,512]{0,1:T(8,128)} fusion(f32[1536,512]{0,1:T(8,128)} %all-gather.7.cloned.1.call-done, f32[3072,1536]{1,0:T(8,128)} %param.8), kind=kOutput, calls=%fused_computation | convolution fusion | flops 14495514624 | bytes 28311552 | tf_op jit(solution)/shard_map/dot_general | solution.py:15
  121.9 6.6 %copy.61 = f32[3072,512]{1,0:T(8,128)} copy(f32[3072,512]{0,1:T(8,128)} %convolution_bitcast_fusion) | data formatting | bytes 12582912 | tf_op jit(solution)/shard_map/dot_general | solution.py:15
  128.5 2.4 dynamic-slice_bitcast_fusion
  130.9 3.3 collective-permute-start.2
  134.2 5.3 %collective-permute-done.2 = f32[2,4,192,512]{3,2,1,0:T(8,128)S(1)} collective-permute-done((f32[2,4,192,512]{3,2,1,0:T(8,128)S(1)}, f32[2,4,192,512]{3,2,1,0:T(8,128)S(1)}, u32[]{:S(2)}, u32[]{:S(2)}) %collective-permute-start.2) | collective-permute-done | bytes 3145760 | tf_op jit(solution)/shard_map/ppermute | solution.py:58
  139.5 0.7 fusion
  140.3 1.9 copy.62
  142.3 1.3 constant_dynamic-slice_fusion
  143.6 1.4 constant_dynamic-slice_fusion.1
  145.0 0.3 copy.66
  145.4 4.6 %collective-permute-start.4 = (f32[192,1024]{1,0:T(8,128)S(1)}, f32[192,1024]{1,0:T(8,128)S(1)}, u32[]{:S(2)}, u32[]{:S(2)}) collective-permute-start(f32[192,1024]{1,0:T(8,128)S(1)} %copy.66), channel_id=1, source_target_pairs={{0,0},{16,1},{32,2},{48,3},{64,4},{80,5},{96,6},{112,7},{1,8},{17,... | collective-permute-start | bytes 2359304 | tf_op jit(solution)/shard_map/ppermute | solution.py:71
  150.0 1.0 dynamic-slice_bitcast_fusion.3
  151.1 0.6 collective-permute-start.1
  151.6 44.6 %reduce-scatter.7.cloned.1.call-done = f32[384,512]{1,0:T(8,128)} async-done(((f32[1536,512]{1,0:T(8,128)}), f32[384,512]{1,0:T(8,128)}) %reduce-scatter.7.cloned.1.call-update) | async-done | bytes 786448 | tf_op jit(solution)/shard_map/reduce_scatter | solution.py:60
  196.3 1.8 dynamic-slice_bitcast_fusion.2
  198.0 4.6 %collective-permute-start.3 = (f32[192,512]{1,0:T(8,128)}, f32[192,512]{1,0:T(8,128)S(1)}, u32[]{:S(2)}, u32[]{:S(2)}) collective-permute-start(f32[192,512]{1,0:T(8,128)} %dynamic-slice_bitcast_fusion.2), channel_id=1, source_target_pairs={{0,8},{8,0},{1,9},{9,1},{2,10},{10,2},{3,11},{11,3},{4,12},{12,4},... | collective-permute-start | bytes 1179656 | tf_op jit(solution)/shard_map/ppermute | solution.py:63
  202.7 1.9 negate_bitcast_fusion
  204.6 7.3 %collective-permute-done.3 = f32[192,512]{1,0:T(8,128)S(1)} collective-permute-done((f32[192,512]{1,0:T(8,128)}, f32[192,512]{1,0:T(8,128)S(1)}, u32[]{:S(2)}, u32[]{:S(2)}) %collective-permute-start.3) | collective-permute-done | bytes 393248 | tf_op jit(solution)/shard_map/ppermute | solution.py:63
  212.0 1.8 fusion.10
  213.8 2.6 fusion.14
  216.4 1.7 fusion.2
  218.1 1.0 collective-permute-start.5
  219.1 3.4 collective-permute-done.5
  222.5 3.4 fusion.4
  226.0 25.9 %reduce-scatter.9.cloned.1.call-done = f32[192,512]{1,0:T(8,128)} async-done(((f32[768,512]{1,0:T(8,128)}), f32[192,512]{1,0:T(8,128)}) %reduce-scatter.9.cloned.1.call-update) | async-done | bytes 393232 | tf_op jit(solution)/shard_map/reduce_scatter | solution.py:81
  252.0 21.8 %reduce-scatter.11.cloned.1.call-done = f32[48,512]{1,0:T(8,128)} async-done(((f32[192,512]{1,0:T(8,128)}), f32[48,512]{1,0:T(8,128)}) %reduce-scatter.11.cloned.1.call-update) | async-done | bytes 98320 | tf_op jit(solution)/shard_map/reduce_scatter | solution.py:82
  273.8 11.9 %all-gather = f32[192,512]{1,0:T(8,128)S(1)} all-gather(f32[48,512]{1,0:T(8,128)} %reduce-scatter.11.cloned.1.call-done), channel_id=2, replica_groups=mesh['xl'=2,'z'=4,'xh'=2,'y'=4,'core'=2] {'xl','xh'}, dimensions={0}, use_global_device_ids=true | all-gather | bytes 491520 | tf_op jit(solution)/shard_map/all_gather | solution.py:83
  285.8 10.6 %all_gather.22 = f32[192,512]{1,0:T(8,128)} all-gather(f32[48,512]{1,0:T(8,128)S(1)} %reduce_sum.9), channel_id=1, replica_groups=mesh['xl'=2,'z'=4,'xh'=2,'y'=4,'core'=2] {'z'}, dimensions={0}, use_global_device_ids=true | all-gather | bytes 491520 | tf_op jit(solution)/shard_map/all_gather | solution.py:84
  296.4 33.3 %all-gather.9.cloned.1.call-done = f32[768,512]{1,0:T(8,128)} async-done(((f32[192,512]{1,0:T(8,128)}), f32[768,512]{1,0:T(8,128)}) %all-gather.9.cloned.1.call-update) | async-done | bytes 1572880 | tf_op jit(solution)/shard_map/all_gather | solution.py:85
  329.6 1.9 copy.68
  331.5 0.9 collective-permute-start.6
  332.4 1.5 fusion.5
  334.0 1.1 pad_maximum_fusion.1
  335.0 1.3 copy.63
  336.3 5.5 %all-to-all-start = ((f32[2,192,512]{1,0,2:T(2,128)}), f32[2,192,512]{1,0,2:T(2,128)}, u32[]{:S(2)}, u32[]{:S(2)}) async-start(f32[2,192,512]{1,0,2:T(2,128)} %copy.63), calls=%async_computation.2 | async-start | bytes 2097152 | tf_op jit(solution)/shard_map/all_to_all | solution.py:101
  341.8 2.5 copy.70
  344.4 2.5 copy.72
  346.9 12.1 %all-to-all-done = f32[2,192,512]{1,0,2:T(2,128)} async-done(((f32[2,192,512]{1,0,2:T(2,128)}), f32[2,192,512]{1,0,2:T(2,128)}, u32[]{:S(2)}, u32[]{:S(2)}) %all-to-all-start) | async-done | bytes 786464 | tf_op jit(solution)/shard_map/all_to_all | solution.py:101
  359.0 1.3 copy.64
  360.3 0.9 fusion.13
  361.2 0.3 copy.65
  361.5 1.0 squeeze.40
  362.5 1.3 copy.71
  363.8 1.0 squeeze.41
  364.8 2.4 maximum_select_fusion
  367.3 1.0 fusion.8
  368.3 1.0 copy-done.4
  369.3 0.2 slice_add_fusion.1
  369.5 2.0 bitcast_subtract_fusion
  371.5 1.3 copy.74
  372.8 2.9 fusion.7
  375.7 1.3 copy.75
  (37 shorter events, 0.7 us)
Async XLA Ops:
  7.2 325.3 %copy-start = (f32[512,512]{1,0:T(8,128)S(1)}, f32[512,512]{1,0:T(8,128)}, u32[]{:S(2)}) copy-start(f32[512,512]{1,0:T(8,128)} %param.11) | copy-start | bytes 3145732
  7.2 48.0 %all-gather.5.cloned.1.call-start = ((), (), s32[]{:S(2)}) async-start(), calls=%async_computation.5 | async-start | bytes 3538944 | tf_op jit(solution)/shard_map/all_gather | solution.py:65
  10.0 91.3 %all-gather.7.cloned.1.call-start = ((), (), s32[]{:S(2)}) async-start(), calls=%async_computation.7 | async-start | bytes 3538944 | tf_op jit(solution)/shard_map/all_gather | solution.py:66
  11.9 138.1 %reduce-scatter.5.cloned.1.call-start = ((), (), s32[]{:S(2)}) async-start(), calls=%async_computation.6 | async-start | bytes 3932160 | tf_op jit(solution)/shard_map/reduce_scatter | solution.py:60
  86.4 8.7 %collective-permute-start = (f32[2,4,192,512]{3,2,1,0:T(8,128)}, f32[2,4,192,512]{3,2,1,0:T(8,128)}, u32[]{:S(2)}, u32[]{:S(2)}) collective-permute-start(f32[2,4,192,512]{3,2,1,0:T(8,128)} %dynamic-slice_bitcast_fusion.1), channel_id=1, source_target_pairs={{0,1},{1,0},{2,3},{3,2},{4,5},{5,4},{6,7},{7,6},{8,9},{9,8},{10,11... | collective-permute-start | bytes 9437192 | tf_op jit(solution)/shard_map/ppermute | solution.py:58
  100.8 95.5 %reduce-scatter.7.cloned.1.call-start = ((), (), s32[]{:S(2)}) async-start(), calls=%async_computation.8 | async-start | bytes 3932160 | tf_op jit(solution)/shard_map/reduce_scatter | solution.py:60
  128.5 11.0 %copy-start.1 = (f32[3072,512]{1,0:T(8,128)S(1)}, f32[3072,512]{1,0:T(8,128)}, u32[]{:S(2)}) copy-start(f32[3072,512]{1,0:T(8,128)} %copy.61) | copy-start | bytes 18874372
  130.9 8.6 %collective-permute-start.2 = (f32[2,4,192,512]{3,2,1,0:T(8,128)S(1)}, f32[2,4,192,512]{3,2,1,0:T(8,128)S(1)}, u32[]{:S(2)}, u32[]{:S(2)}) collective-permute-start(f32[2,4,192,512]{3,2,1,0:T(8,128)S(1)} %dynamic-slice_bitcast_fusion), channel_id=1, source_target_pairs={{0,1},{1,0},{2,3},{3,2},{4,5},{5,4},{6,7},{7,6},{8,9},{9,8},{10,11... | collective-permute-start | bytes 9437192 | tf_op jit(solution)/shard_map/ppermute | solution.py:58
  142.2 109.7 %reduce-scatter.9.cloned.1.call-start = ((), (), s32[]{:S(2)}) async-start(), calls=%async_computation.9 | async-start | bytes 1966080 | tf_op jit(solution)/shard_map/reduce_scatter | solution.py:81
  145.4 59.2 %collective-permute-start.4 = (f32[192,1024]{1,0:T(8,128)S(1)}, f32[192,1024]{1,0:T(8,128)S(1)}, u32[]{:S(2)}, u32[]{:S(2)}) collective-permute-start(f32[192,1024]{1,0:T(8,128)S(1)} %copy.66), channel_id=1, source_target_pairs={{0,0},{16,1},{32,2},{48,3},{64,4},{80,5},{96,6},{112,7},{1,8},{17,... | collective-permute-start | bytes 2359304 | tf_op jit(solution)/shard_map/ppermute | solution.py:71
  151.1 51.6 %collective-permute-start.1 = (f32[192,512]{1,0:T(8,128)S(1)}, f32[192,512]{1,0:T(8,128)}, u32[]{:S(2)}, u32[]{:S(2)}) collective-permute-start(f32[192,512]{1,0:T(8,128)S(1)} %dynamic-slice_bitcast_fusion.3), channel_id=1, source_target_pairs={{0,8},{8,0},{1,9},{9,1},{2,10},{10,2},{3,11},{11,3},{4,12},{12,4},... | collective-permute-start | bytes 1179656 | tf_op jit(solution)/shard_map/ppermute | solution.py:63
  198.0 13.9 %collective-permute-start.3 = (f32[192,512]{1,0:T(8,128)}, f32[192,512]{1,0:T(8,128)S(1)}, u32[]{:S(2)}, u32[]{:S(2)}) collective-permute-start(f32[192,512]{1,0:T(8,128)} %dynamic-slice_bitcast_fusion.2), channel_id=1, source_target_pairs={{0,8},{8,0},{1,9},{9,1},{2,10},{10,2},{3,11},{11,3},{4,12},{12,4},... | collective-permute-start | bytes 1179656 | tf_op jit(solution)/shard_map/ppermute | solution.py:63
  204.6 9.2 %copy-start.5 = (f32[192,1024]{1,0:T(8,128)}, f32[192,1024]{1,0:T(8,128)S(1)}, u32[]{:S(2)}) copy-start(f32[192,1024]{1,0:T(8,128)S(1)} %collective-permute-done.4) | copy-start | bytes 2359300
  212.0 1.8 copy-start.6
  213.8 4.3 %copy-start.3 = (f32[512,512]{1,0:T(8,128)}, f32[512,512]{1,0:T(8,128)S(1)}, u32[]{:S(2)}) copy-start(f32[512,512]{1,0:T(8,128)S(1)} %fusion.10) | copy-start | bytes 3145732
  218.1 4.4 %collective-permute-start.5 = (f32[768,512]{1,0:T(8,128)}, f32[768,512]{1,0:T(8,128)}, u32[]{:S(2)}, u32[]{:S(2)}) collective-permute-start(f32[768,512]{1,0:T(8,128)} %fusion.2), channel_id=1, source_target_pairs={{0,1},{1,0},{2,3},{3,2},{4,5},{5,4},{6,7},{7,6},{8,9},{9,8},{10,11... | collective-permute-start | bytes 4718600 | tf_op jit(solution)/shard_map/ppermute | solution.py:80
  225.9 106.5 %copy-start.7 = (f32[192,512]{1,0:T(8,128)S(1)}, f32[192,512]{1,0:T(8,128)}, u32[]{:S(2)}) copy-start(f32[192,512]{1,0:T(8,128)} %copy-done.6) | copy-start | bytes 1179652
  225.9 47.9 %reduce-scatter.11.cloned.1.call-start = ((), (), s32[]{:S(2)}) async-start(), calls=%async_computation.10 | async-start | bytes 491520 | tf_op jit(solution)/shard_map/reduce_scatter | solution.py:82
  251.9 77.7 %all-gather.9.cloned.1.call-start = ((), (), s32[]{:S(2)}) async-start(), calls=%async_computation.11 | async-start | bytes 1966080 | tf_op jit(solution)/shard_map/all_gather | solution.py:85
  331.5 33.3 %collective-permute-start.6 = (f32[768,512]{0,1:T(8,128)S(1)}, f32[768,512]{0,1:T(8,128)}, u32[]{:S(2)}, u32[]{:S(2)}) collective-permute-start(f32[768,512]{0,1:T(8,128)S(1)} %copy.68), channel_id=1, source_target_pairs={{0,1},{1,0},{2,3},{3,2},{4,5},{5,4},{6,7},{7,6},{8,9},{9,8},{10,11... | collective-permute-start | bytes 4718600 | tf_op jit(solution)/shard_map/ppermute | solution.py:86
  336.3 22.7 %all-to-all-start = ((f32[2,192,512]{1,0,2:T(2,128)}), f32[2,192,512]{1,0,2:T(2,128)}, u32[]{:S(2)}, u32[]{:S(2)}) async-start(f32[2,192,512]{1,0,2:T(2,128)} %copy.63), calls=%async_computation.2 | async-start | bytes 2097152 | tf_op jit(solution)/shard_map/all_to_all | solution.py:101
  367.2 2.2 copy-start.2
  367.3 2.0 copy-start.4
Sparse Core Ops, SparseCore 0:
  10.2 44.9 all-gather.4
  57.4 43.7 all-gather.6
  103.7 40.2 reduce-scatter.4
  146.2 49.9 reduce-scatter.6
  226.1 25.7 reduce-scatter.8
  254.1 19.6 reduce-scatter.10
  296.5 33.1 all-gather.8
